TPU v7x, 32 devices: a whole 2x2x4 slice. The times are simulated.
32 devices in a mesh: groups: 2 (over y), seq: 4 (over z), head: 4 (over x, core).
Axes of the slice: x: 2, y: 2, z: 4, core: 2. Of those that a mesh axis runs over, the one named last changes fastest.
Arguments:
- x_in: bfloat16 [1024, 8192], P(('groups', 'seq'), 'head'), parts along dimension 0, may hold values from -6 to 6
- bc_in: bfloat16 [1024, 8, 256], P(('groups', 'seq'), 'head'), parts along dimension 0, may hold values from -6 to 6
- z_in: bfloat16 [1024, 8192], P(('groups', 'seq'), 'head'), parts along dimension 0, may hold values from -6 to 6
- dt_raw: float32 [1024, 128], P(('groups', 'seq'), 'head'), parts along dimension 0, may hold values from -12 to 0
- conv_x: float32 [4, 8192], P(None, 'head'), may hold values from -3 to 3
- conv_bc: float32 [4, 8, 256], P(None, 'head'), may hold values from -3 to 3
- a_log: float32 [128], P('head'), may hold values from -0.35 to 0.35
- d_skip: float32 [128], P('head'), may hold values from 0.5 to 1.5
- norm_gain: float32 [8192], P('head'), may hold values from 0.25 to 1.75
Outputs:
- out: bfloat16 [1024, 8192], P(('groups', 'seq'), 'head'), parts along dimension 0
There are 2 independent parts, one for each index of `groups`. A program takes and returns all parts, laid end to end along the dimension named above; an argument that names none is the same for every part. Nothing has to cross between parts.
All inputs are finite; a program needn't handle non-finite values.
Results may differ from a plain program's by a relative error of at most 0.0056.
Values may be sent and summed in bfloat16 or wider, within the bound.
A program may use at most 192 MiB of HBM per device.

v0:
```python
import jax
import jax.numpy as jnp
from jax import lax
from jax.sharding import PartitionSpec as P

CONV = 4
BLOCK = 128


EPS = 1e-05


def passed_along(block, axis, distance):
    devices = range(lax.axis_size(axis))
    route = [(i - distance, i) for i in devices if i - distance in devices]
    return lax.ppermute(block, axis, route)


def conv_silu(tail_rows, series, taps):
    length = series.shape[0]
    padded = jnp.concatenate([tail_rows.astype(jnp.float32), series.astype(jnp.float32)], axis=0)
    running = jnp.zeros(series.shape, jnp.float32)
    for offset in range(taps.shape[0]):
        running = running + taps[offset] * padded[offset : offset + length]
    return jax.nn.silu(running).astype(jnp.bfloat16)


def block_terms(inputs, b_input, c_output, deltas, rates):
    cum_rate = jnp.cumsum(rates, axis=0)
    cum_moved = jnp.transpose(cum_rate, (1, 2, 0))
    delta_moved = jnp.transpose(deltas, (1, 2, 0))
    places = jnp.arange(cum_rate.shape[0])
    causal = places[:, None] >= places[None, :]
    gaps_all = cum_moved[..., :, None] - cum_moved[..., None, :]
    decays = jnp.where(causal, jnp.exp(jnp.where(causal, gaps_all, 0.0)), 0.0)
    intersection = jnp.einsum("tgn,sgn->gts", c_output, b_input, preferred_element_type=jnp.float32)
    weight = (decays * delta_moved[..., None, :] * intersection[:, None]).astype(jnp.bfloat16)
    y_intra = jnp.einsum("ghts,sghp->tghp", weight, inputs, preferred_element_type=jnp.float32)
    tail_decay = jnp.exp(cum_rate[-1] - cum_rate) * deltas
    scaled = (tail_decay[..., None] * inputs.astype(jnp.float32)).astype(jnp.bfloat16)
    states = jnp.einsum("sghp,sgn->ghpn", scaled, b_input, preferred_element_type=jnp.float32)
    return (y_intra, states, cum_rate, jnp.exp(cum_rate[-1]))


def block_output(y_intra, cum_rate, c_output, inputs, gates, incoming, skip, gain):
    state_half = incoming.astype(jnp.bfloat16)
    from_state = jnp.einsum(
        "tgn,ghpn->tghp", c_output, state_half, preferred_element_type=jnp.float32
    )
    mixed = (
        y_intra
        + jnp.exp(cum_rate)[..., None] * from_state
        + skip[..., None] * inputs.astype(jnp.float32)
    )
    gated = mixed * jax.nn.silu(gates.astype(jnp.float32))
    mean_sq = jnp.mean(gated * gated, axis=(2, 3), keepdims=True)
    return (gated * lax.rsqrt(mean_sq + EPS) * gain).astype(jnp.bfloat16)


def summarize(carry, piece):
    block_decay, states = piece
    return ((carry[0] * block_decay, block_decay[..., None, None] * carry[1] + states), None)


def advance_rows(carry, piece):
    return (piece[0] * carry + piece[1], carry)


def shards(x_in, bc_in, z_in, dt_raw, conv_x, conv_bc, a_log, d_skip, norm_gain):
    rim = CONV - 1
    tokens = x_in.shape[0]
    groups_dev = bc_in.shape[1]
    heads_dev = dt_raw.shape[1]
    per_group = heads_dev // groups_dev
    state_dim = bc_in.shape[2] // 2
    head_dim = x_in.shape[1] // heads_dev
    width_x = x_in.shape[1]
    last_rows = jnp.concatenate(
        [x_in[tokens - rim :], bc_in[tokens - rim :].reshape(rim, groups_dev * 2 * state_dim)],
        axis=1,
    )
    got_rows = passed_along(last_rows, "seq", 1)
    x_act = conv_silu(got_rows[:, :width_x], x_in, conv_x)
    bc_act = conv_silu(
        got_rows[:, width_x:].reshape(rim, groups_dev, 2 * state_dim), bc_in, conv_bc
    )
    deltas = jax.nn.softplus(dt_raw)
    rates = -jnp.exp(a_log)[None, :] * deltas
    block_count = tokens // BLOCK
    inputs = x_act.reshape(block_count, BLOCK, groups_dev, per_group, head_dim)
    b_input = bc_act[:, :, :state_dim].reshape(block_count, BLOCK, groups_dev, state_dim)
    c_output = bc_act[:, :, state_dim:].reshape(block_count, BLOCK, groups_dev, state_dim)
    delta_blocks = deltas.reshape(block_count, BLOCK, groups_dev, per_group)
    rate_blocks = rates.reshape(block_count, BLOCK, groups_dev, per_group)
    y_intra, states, cum_rate, block_decay = jax.vmap(block_terms)(
        inputs, b_input, c_output, delta_blocks, rate_blocks
    )
    start_decay = jnp.ones((groups_dev, per_group), jnp.float32)
    start_state = jnp.zeros((groups_dev, per_group, head_dim, state_dim), jnp.float32)
    summary, _ = lax.scan(summarize, (start_decay, start_state), (block_decay, states))
    decay_dev, states_dev = summary
    seq_count = lax.axis_size("seq")
    width_block = states_dev.size // seq_count
    flat_states = states_dev.reshape(seq_count, width_block)
    decay_rows = jnp.broadcast_to(decay_dev.reshape(1, heads_dev), (seq_count, heads_dev))
    got_states, got_decays = (
        lax.all_to_all(flat_states, "seq", split_axis=0, concat_axis=0, tiled=True),
        lax.all_to_all(decay_rows, "seq", split_axis=0, concat_axis=0, tiled=True),
    )
    owner = (lax.axis_index("seq") * width_block + jnp.arange(width_block, dtype=jnp.int32)) // (
        head_dim * state_dim
    )
    select = (owner[:, None] == jnp.arange(heads_dev, dtype=jnp.int32)[None, :]).astype(jnp.float32)
    entry_decay = jnp.dot(got_decays, select.T, precision=lax.Precision.HIGHEST)
    _, before = lax.scan(
        advance_rows, jnp.zeros((width_block,), jnp.float32), (entry_decay, got_states)
    )
    incoming = lax.all_to_all(before, "seq", split_axis=0, concat_axis=0, tiled=True).reshape(
        states_dev.shape
    )
    gates = z_in.reshape(block_count, BLOCK, groups_dev, per_group, head_dim)
    skip = d_skip.reshape(groups_dev, per_group)
    gain = norm_gain.reshape(groups_dev, per_group, head_dim)

    def emit(carry, piece):
        y_part, state_part, cum_part, decay_part, c_part, input_part, gate_part = piece
        result = block_output(y_part, cum_part, c_part, input_part, gate_part, carry, skip, gain)
        return (decay_part[..., None, None] * carry + state_part, result)

    _, outputs = lax.scan(
        emit, incoming, (y_intra, states, cum_rate, block_decay, c_output, inputs, gates)
    )
    return outputs.reshape(tokens, width_x)


def solution(mesh):
    return jax.shard_map(
        shards,
        mesh=mesh,
        in_specs=(
            P(("groups", "seq"), "head"),
            P(("groups", "seq"), "head", None),
            P(("groups", "seq"), "head"),
            P(("groups", "seq"), "head"),
            P(None, "head"),
            P(None, "head", None),
            P("head"),
            P("head"),
            P("head"),
        ),
        out_specs=P(("groups", "seq"), "head"),
        check_vma=False,
    )
```

profile of v0, /device:TPU:0, one launch (start us, length us, event | category | flops | bytes accessed | tf_op | source)
XLA Modules:
  0.0 104.4 jit_solution(37182162923625253)
XLA Ops:
  0.0 0.8 slice.65
  0.8 0.7 slice_bitcast_fusion
  1.6 5.0 %collective-permute-start = (bf16[3,2560]{1,0:T(4,128)(2,1)S(1)}, bf16[3,2560]{1,0:T(4,128)(2,1)S(1)}, u32[]{:S(2)}, u32[]{:S(2)}) collective-permute-start(bf16[3,2560]{1,0:T(4,128)(2,1)S(1)} %pad_maximum_fusion.2), channel_id=1, source_target_pairs={{0,4},{4,8},{8,12},{1,5},{5,9},{9,13},{2,6},{6,10},{10,14},{3,7},{... | collective-permute-start | bytes 46088 | tf_op jit(solution)/shard_map/ppermute | solution.py:16
  6.5 0.7 exponential_negate_fusion
  7.2 0.8 broadcast_multiply_fusion
  8.0 0.1 copy.64
  8.1 0.1 fusion.45
  8.2 0.1 exp.68
  8.3 0.6 broadcast_in_dim.57
  8.9 3.9 %all-to-all-start = ((f32[4,1,32]{2,1,0:T(1,128)}), f32[4,1,32]{2,1,0:T(1,128)S(1)}, u32[]{:S(2)}, u32[]{:S(2)}) async-start(f32[4,1,32]{2,1,0:T(1,128)} %broadcast_in_dim.57), calls=%async_computation | async-start | bytes 4096 | tf_op jit(solution)/shard_map/all_to_all | solution.py:108
  12.8 0.9 copy_convert_fusion
  13.7 0.1 copy.68
  13.8 0.6 bitcast_exponential_fusion
  14.5 0.1 convert_element_type.61
  14.6 0.0 collective-permute-done
  14.6 0.7 multiply_convert_fusion.3
  15.3 0.3 copy.63
  15.5 0.0 copy-start
  15.6 0.2 multiply_convert_fusion.4
  15.8 1.3 %convolution_add_fusion = f32[2,16,64,128]{3,2,1,0:T(8,128)} fusion(bf16[128,2,16,64]{0,3,2,1:T(8,128)(2,1)S(1)} %bitcast.91, f32[128,2,16]{0,2,1:T(8,128)S(1)} %get-tuple-element.123, f32[2,16]{1,0:T(2,128)S(1)} %exponential_multiply_fusion, bf16[128,2,256]{2,0,1:T(8,128)(2,1)S(1)} %multiply_convert_fusion.4), kind=kOutput, calls=%fused_computation.15 | convolution fusion | flops 68157440 | bytes 1655808 | tf_op jit(solution)/shard_map/vmap(sghp,sgn->ghpn)/dot_general | solution.py:41
  17.0 1.2 %all-to-all-done = f32[4,1,32]{2,1,0:T(1,128)S(1)} async-done(((f32[4,1,32]{2,1,0:T(1,128)}), f32[4,1,32]{2,1,0:T(1,128)S(1)}, u32[]{:S(2)}, u32[]{:S(2)}) %all-to-all-start) | async-done | bytes 544 | tf_op jit(solution)/shard_map/all_to_all | solution.py:108
  18.2 3.9 %all-to-all-start.1 = ((f32[4,1,65536]{2,1,0:T(1,128)}), f32[4,1,65536]{2,1,0:T(1,128)S(1)}, u32[]{:S(2)}, u32[]{:S(2)}) async-start(f32[4,1,65536]{2,1,0:T(1,128)} %bitcast.26), calls=%async_computation.1 | async-start | bytes 2097152 | tf_op jit(solution)/shard_map/all_to_all | solution.py:107
  22.1 0.2 add_select_fusion
  22.3 2.6 %fusion = f32[4,65536]{1,0:T(4,128)S(1)} fusion(f32[4,32]{1,0:T(4,128)S(1)} %bitcast.106, s32[65536]{0:T(1024)S(1)} %add_select_fusion), kind=kOutput, calls=%fused_computation.5 | convolution fusion | flops 102760448 | bytes 1311232 | tf_op jit(solution)/shard_map/dot_general | solution.py:114
  24.9 22.1 %all-to-all-done.1 = f32[4,1,65536]{2,1,0:T(1,128)S(1)} async-done(((f32[4,1,65536]{2,1,0:T(1,128)}), f32[4,1,65536]{2,1,0:T(1,128)S(1)}, u32[]{:S(2)}, u32[]{:S(2)}) %all-to-all-start.1) | async-done | bytes 1048608 | tf_op jit(solution)/shard_map/all_to_all | solution.py:107
  47.0 0.7 copy.78
  47.7 24.1 %while.3 = (s32[]{:T(128)}, f32[65536]{0:T(1024)S(1)}, bf16[4,65536]{1,0:T(4,128)(2,1)}, f32[4,65536]{1,0:T(4,128)S(1)}, f32[4,65536]{1,0:T(4,128)S(1)}, /*index=5*/s32[]{:T(128)}, s32[]{:T(128)}) while((s32[]{:T(128)}, f32[65536]{0:T(1024)S(1)}, bf16[4,65536]{1,0:T(4,128)(2,1)}, f32[4,65536]{1,0:T(4,128)S(1)}, ...), condition=%wide.region_2.3_spmd.clone, body=%wide.region_1.2_spmd.clone.sunk | while | flops 196611 | bytes 2883679 | solution.py:115
  47.7 0.5 constant_dynamic-slice_fusion.3
  48.3 0.2 multiply_add_fusion.2
  48.4 5.3 %dynamic_update_slice.9 = bf16[4,65536]{1,0:T(4,128)(2,1)} dynamic-update-slice(bf16[4,65536]{1,0:T(4,128)(2,1)} %get-tuple-element.180, f32[1,65536]{1,0:T(1,128)S(1)} %bitcast.87, s32[]{:T(128)} %get-tuple-element.178, s32[]{:T(128)} %constant.78.clone.1..sunk) | dynamic-update-slice | bytes 524292 | tf_op jit(solution)/shard_map/while/body/jit(dynamic_update_index_in_dim)/dynamic_update_slice | solution.py:115
  53.8 0.5 constant_dynamic-slice_fusion.3
  54.3 0.2 multiply_add_fusion.2
  54.5 5.3 %dynamic_update_slice.9 = bf16[4,65536]{1,0:T(4,128)(2,1)} dynamic-update-slice(bf16[4,65536]{1,0:T(4,128)(2,1)} %get-tuple-element.180, f32[1,65536]{1,0:T(1,128)S(1)} %bitcast.87, s32[]{:T(128)} %get-tuple-element.178, s32[]{:T(128)} %constant.78.clone.1..sunk) | dynamic-update-slice | bytes 524292 | tf_op jit(solution)/shard_map/while/body/jit(dynamic_update_index_in_dim)/dynamic_update_slice | solution.py:115
  59.8 0.5 constant_dynamic-slice_fusion.3
  60.3 0.2 multiply_add_fusion.2
  60.5 5.3 %dynamic_update_slice.9 = bf16[4,65536]{1,0:T(4,128)(2,1)} dynamic-update-slice(bf16[4,65536]{1,0:T(4,128)(2,1)} %get-tuple-element.180, f32[1,65536]{1,0:T(1,128)S(1)} %bitcast.87, s32[]{:T(128)} %get-tuple-element.178, s32[]{:T(128)} %constant.78.clone.1..sunk) | dynamic-update-slice | bytes 524292 | tf_op jit(solution)/shard_map/while/body/jit(dynamic_update_index_in_dim)/dynamic_update_slice | solution.py:115
  65.8 0.5 constant_dynamic-slice_fusion.3
  66.4 0.2 multiply_add_fusion.2
  66.5 5.3 %dynamic_update_slice.9 = bf16[4,65536]{1,0:T(4,128)(2,1)} dynamic-update-slice(bf16[4,65536]{1,0:T(4,128)(2,1)} %get-tuple-element.180, f32[1,65536]{1,0:T(1,128)S(1)} %bitcast.87, s32[]{:T(128)} %get-tuple-element.178, s32[]{:T(128)} %constant.78.clone.1..sunk) | dynamic-update-slice | bytes 524292 | tf_op jit(solution)/shard_map/while/body/jit(dynamic_update_index_in_dim)/dynamic_update_slice | solution.py:115
  71.9 1.6 %all_to_all.22 = bf16[4,1,65536]{2,1,0:T(2,128)(2,1)S(1)} reshape(bf16[4,65536]{1,0:T(4,128)(2,1)} %get-tuple-element.69) | data formatting | bytes 1048576 | tf_op jit(solution)/shard_map/all_to_all | solution.py:118
  73.4 0.6 broadcast.125
  74.0 4.0 %reduce.2 = bf16[4,65536]{1,0:T(4,128)(2,1)S(1)} reduce(bf16[4,1,65536]{2,1,0:T(2,128)(2,1)S(1)} %all_to_all.22, bf16[]{:T(256)} %broadcast.125), dimensions={1}, to_apply=%all_to_all.22.reduce_sub_computation | reduce | bytes 1048578 | tf_op jit(solution)/shard_map/all_to_all | solution.py:118
  78.0 0.0 copy-start.5
  78.0 1.4 %reshape.194 = bf16[4,2,32768]{2,1,0:T(2,128)(2,1)} reshape(bf16[4,65536]{1,0:T(4,128)(2,1)S(1)} %reduce.2) | data formatting | bytes 1048576
  79.4 3.6 %all-to-all-start.2 = ((bf16[4,2,32768]{2,1,0:T(2,128)(2,1)}), bf16[4,2,32768]{2,1,0:T(2,128)(2,1)S(1)}, u32[]{:S(2)}, u32[]{:S(2)}) async-start(bf16[4,2,32768]{2,1,0:T(2,128)(2,1)} %reshape.194), calls=%async_computation.2 | async-start | bytes 1048576 | tf_op jit(solution)/shard_map/all_to_all | solution.py:118
  83.1 0.0 copy-start.10
  83.1 0.0 copy-start.8
  83.1 0.0 copy-start.1
  83.1 0.1 copy.65
  83.2 0.2 copy.70
  83.4 0.3 copy-done.10
  83.7 0.1 mul.275
  83.8 0.1 mul.283
  83.9 0.1 copy-done.3
  84.0 0.2 fusion.37
  84.2 0.0 copy-done.1
  84.2 1.9 %convolution_bitcast_fusion.1 = f32[128,2,16,64]{0,3,2,1:T(8,128)} fusion(bf16[128,2,16,64]{0,3,2,1:T(8,128)(2,1)S(1)} %bitcast.92, f32[2,128,128]{2,1,0:T(8,128)S(1)} %fusion.37, f32[2,16,128]{2,1,0:T(8,128)S(1)} %bitcast.99, f32[2,16,128]{2,1,0:T(8,128)S(1)} %copy.65, pred[128,128]{1,0:T(8,128)(4,1)S(1)} %iota_compare_fusion.2), kind=kOutput, calls=%fused_computation.16 | convolution fusion | flops 70254592 | bytes 1753088 | tf_op jit(solution)/shard_map/vmap(ghts,sghp->tghp)/dot_general | solution.py:38
  86.1 10.8 %all-to-all-done.2 = bf16[4,2,32768]{2,1,0:T(2,128)(2,1)S(1)} async-done(((bf16[4,2,32768]{2,1,0:T(2,128)(2,1)}), bf16[4,2,32768]{2,1,0:T(2,128)(2,1)S(1)}, u32[]{:S(2)}, u32[]{:S(2)}) %all-to-all-start.2) | async-done | bytes 524320 | tf_op jit(solution)/shard_map/all_to_all | solution.py:118
  96.9 0.5 reshape.195
  97.4 3.2 %convert_reduce_fusion = bf16[4,65536]{1,0:T(4,128)(2,1)S(1)} fusion(bf16[4,1,65536]{2,1,0:T(2,128)(2,1)S(1)} %reshape.195), kind=kLoop, calls=%fused_computation.34 | loop fusion | bytes 1048576 | tf_op jit(solution)/shard_map/while/body/eval_jaxpr/convert_element_type | solution.py:46
  100.7 0.5 convert_element_type.71
  101.2 1.8 %multiply_reduce_fusion = (f32[128,2]{0,1:T(2,128)S(1)}, f32[128,2,16,64]{0,3,2,1:T(8,128)S(1)}) fusion(f32[128,2,16,64]{0,3,2,1:T(8,128)S(1)} %bitcast.96, bf16[128,2,16,64]{0,3,2,1:T(8,128)(2,1)S(1)} %bitcast.93, f32[2,16]{1,0:T(2,128)S(1)} %mul.275, f32[128,2,16,64]{0,3,2,1:T(8,128)} %convolution_bitcast_fusion.1, ...), kind=kOutput, calls=%fused_computation.33 | convolution fusion | flops 70254336 | bytes 4278272 | tf_op jit(solution)/shard_map/while/body/eval_jaxpr/tgn,ghpn->tghp/dot_general | solution.py:47
  103.0 0.3 multiply_convert_fusion.2
  103.4 1.0 copy.71
  (27 shorter events, 0.1 us)
Async XLA Ops:
  0.0 14.5 %copy-start.4 = (bf16[128,2048]{1,0:T(8,128)(2,1)S(1)}, bf16[128,2048]{1,0:T(8,128)(2,1)}, u32[]{:S(2)}) copy-start(bf16[128,2048]{1,0:T(8,128)(2,1)} %param.11) | copy-start | bytes 1572868
  0.0 13.8 %copy-start.6 = (f32[4,2048]{1,0:T(4,128)S(1)}, f32[4,2048]{1,0:T(4,128)}, u32[]{:S(2)}) copy-start(f32[4,2048]{1,0:T(4,128)} %param.15) | copy-start | bytes 98308
  0.0 13.8 %copy-start.9 = (f32[4,2,256]{2,1,0:T(2,128)S(1)}, f32[4,2,256]{2,1,0:T(2,128)}, u32[]{:S(2)}) copy-start(f32[4,2,256]{2,1,0:T(2,128)} %param.16) | copy-start | bytes 24580
  1.6 13.0 %collective-permute-start = (bf16[3,2560]{1,0:T(4,128)(2,1)S(1)}, bf16[3,2560]{1,0:T(4,128)(2,1)S(1)}, u32[]{:S(2)}, u32[]{:S(2)}) collective-permute-start(bf16[3,2560]{1,0:T(4,128)(2,1)S(1)} %pad_maximum_fusion.2), channel_id=1, source_target_pairs={{0,4},{4,8},{8,12},{1,5},{5,9},{9,13},{2,6},{6,10},{10,14},{3,7},{... | collective-permute-start | bytes 46088 | tf_op jit(solution)/shard_map/ppermute | solution.py:16
  8.9 9.3 %all-to-all-start = ((f32[4,1,32]{2,1,0:T(1,128)}), f32[4,1,32]{2,1,0:T(1,128)S(1)}, u32[]{:S(2)}, u32[]{:S(2)}) async-start(f32[4,1,32]{2,1,0:T(1,128)} %broadcast_in_dim.57), calls=%async_computation | async-start | bytes 4096 | tf_op jit(solution)/shard_map/all_to_all | solution.py:108
  15.5 1.5 %copy-start = (bf16[128,2048]{0,1:T(8,128)(2,1)}, bf16[128,2048]{0,1:T(8,128)(2,1)S(1)}, u32[]{:S(2)}) copy-start(bf16[128,2048]{0,1:T(8,128)(2,1)S(1)} %copy.63) | copy-start | bytes 1572868
  15.7 2.5 %copy-start.2 = (bf16[128,2,256]{2,0,1:T(8,128)(2,1)}, bf16[128,2,256]{2,0,1:T(8,128)(2,1)S(1)}, u32[]{:S(2)}) copy-start(bf16[128,2,256]{2,0,1:T(8,128)(2,1)S(1)} %multiply_convert_fusion.4) | copy-start | bytes 393220
  18.2 28.8 %all-to-all-start.1 = ((f32[4,1,65536]{2,1,0:T(1,128)}), f32[4,1,65536]{2,1,0:T(1,128)S(1)}, u32[]{:S(2)}, u32[]{:S(2)}) async-start(f32[4,1,65536]{2,1,0:T(1,128)} %bitcast.26), calls=%async_computation.1 | async-start | bytes 2097152 | tf_op jit(solution)/shard_map/all_to_all | solution.py:107
  78.0 5.2 %copy-start.5 = (bf16[128,2048]{1,0:T(8,128)(2,1)S(1)}, bf16[128,2048]{1,0:T(8,128)(2,1)}, u32[]{:S(2)}) copy-start(bf16[128,2048]{1,0:T(8,128)(2,1)} %param.13) | copy-start | bytes 1572868
  79.4 17.5 %all-to-all-start.2 = ((bf16[4,2,32768]{2,1,0:T(2,128)(2,1)}), bf16[4,2,32768]{2,1,0:T(2,128)(2,1)S(1)}, u32[]{:S(2)}, u32[]{:S(2)}) async-start(bf16[4,2,32768]{2,1,0:T(2,128)(2,1)} %reshape.194), calls=%async_computation.2 | async-start | bytes 1048576 | tf_op jit(solution)/shard_map/all_to_all | solution.py:118
  83.1 0.7 copy-start.10
  83.1 0.7 copy-start.8
  83.1 0.9 copy-start.3
  83.1 1.1 %copy-start.1 = (bf16[128,2048]{0,1:T(8,128)(2,1)S(1)}, bf16[128,2048]{0,1:T(8,128)(2,1)}, u32[]{:S(2)}) copy-start(bf16[128,2048]{0,1:T(8,128)(2,1)} %copy-done) | copy-start | bytes 1572868
  97.4 3.8 %copy-start.7 = (f32[128,2,16]{0,2,1:T(8,128)S(1)}, f32[128,2,16]{0,2,1:T(8,128)}, u32[]{:S(2)}) copy-start(f32[128,2,16]{0,2,1:T(8,128)} %get-tuple-element.122) | copy-start | bytes 49156
where the time goes:
time: 106 us; the launch traced here: 104 us
  local copies, waits for them, and re-layouts  36.6 us (35%)
  waiting for transfers between devices  34 us (32%)
  starting transfers between devices  16.4 us (15%)
  other arithmetic  9.25 us (9%)
  matrix products  7.77 us (7%)
    all_to_all x1, waiting for transfers between devices, shards(): lax.all_to_all(flat_states, 'seq', split_axis=0, concat_axis=0, tiled=True)  22.1 us
    dynamic_update_slice x4, local copies, waits for them, and re-layouts, shards(): lax.scan(advance_rows, jnp.zeros((width_block,), jnp.float32), (entry_dec...  21.3 us
    all_to_all x1, waiting for transfers between devices, shards(): lax.all_to_all(before, 'seq', split_axis=0, concat_axis=0, tiled=True)  10.8 us
    ppermute x1, starting transfers between devices, passed_along(): return lax.ppermute(block, axis, route)  4.96 us
    all_to_all x1, other arithmetic, shards(): lax.all_to_all(before, 'seq', split_axis=0, concat_axis=0, tiled=True)  4 us
    all_to_all x1, starting transfers between devices, shards(): lax.all_to_all(flat_states, 'seq', split_axis=0, concat_axis=0, tiled=True)  3.94 us
    all_to_all x1, starting transfers between devices, shards(): lax.all_to_all(decay_rows, 'seq', split_axis=0, concat_axis=0, tiled=True)  3.86 us
    unnamed x27, local copies, waits for them, and re-layouts  3.8 us
  transfers between devices with their start and end apart: 4, of which 3 were waited for; matrix products, arithmetic and copies ran while one was open for 11% of the time, Pallas kernels for 0%

commit v1 on v0

v1 whole, which is shorter than its diff:
```python
import functools

import jax
import jax.numpy as jnp
from jax import lax
from jax.experimental import pallas as pl
from jax.experimental.pallas import tpu as pltpu
from jax.sharding import PartitionSpec as P

BLOCK = 128
EPS = 1e-05
HALO = 16
HEADS_PER_CHUNK = 4
F32 = jnp.float32
BF16 = jnp.bfloat16
MESH = pl.DeviceIdType.MESH


def silu(v):
    half = 0.5 * v
    return half + half * jnp.tanh(half)


def kernel(
    n, groups, heads, x_ref, bc_ref, z_ref, dt_ref, cx_ref, cbc_ref, al_ref, ds_ref, gain_ref,
    o_ref, xh, bh, sendb, recvb, own, gated, ec, xs, bs, xact, cum_t, dt_t, col_cum, col_tail,
    pad, inter, c_act, b_t, h_send, h_recv, s_send, s_recv,
):
    tokens, width = x_ref.shape
    head_dim = width // heads
    per_chunk = xact.shape[2] // head_dim
    wide = xact.shape[2]
    chunks = width // wide
    group_chunks = chunks // groups
    state = bc_ref.shape[1] // groups // 2
    taps = cx_ref.shape[0]
    base = 8 - (taps - 1)
    me = lax.axis_index("seq")

    def halo_copies():
        rows = pl.ds(tokens - HALO, HALO)
        return [
            pltpu.make_async_remote_copy(
                src_ref=src.at[rows], dst_ref=dst, send_sem=h_send.at[i], recv_sem=h_recv.at[i],
                device_id={"seq": me + 1}, device_id_type=MESH,
            )
            for i, (src, dst) in enumerate(((bc_ref, bh), (x_ref, xh)))
        ]

    def state_copy(k):
        return pltpu.make_async_remote_copy(
            src_ref=sendb.at[k], dst_ref=recvb.at[k], send_sem=s_send.at[k],
            recv_sem=s_recv.at[k], device_id={"seq": me + 1}, device_id_type=MESH,
        )

    barrier = pltpu.get_barrier_semaphore()

    @pl.when(me > 0)
    def _():
        pl.semaphore_signal(barrier, inc=1, device_id={"seq": me - 1}, device_id_type=MESH)

    @pl.when(me < n - 1)
    def _():
        pl.semaphore_wait(barrier, 1)
        for copy in halo_copies():
            copy.start()

    row = lax.broadcasted_iota(jnp.int32, (tokens, tokens), 0)
    col = lax.broadcasted_iota(jnp.int32, (tokens, tokens), 1)
    causal = row >= col
    raw = dt_ref[...]
    deltas = jnp.maximum(raw, 0.0) + jnp.log1p(jnp.exp(-jnp.abs(raw)))
    rates = -jnp.exp(al_ref[...]) * deltas
    cum = jnp.dot(
        causal.astype(F32), rates, precision=lax.Precision.HIGHEST, preferred_element_type=F32
    )
    tail = jnp.exp(cum[tokens - 1 : tokens] - cum) * deltas
    for k in range(chunks):
        part = slice(k * per_chunk, (k + 1) * per_chunk)
        col_cum[k] = cum[:, part]
        col_tail[k] = tail[:, part]
    pad[...] = jnp.zeros_like(pad)
    pad[:, :heads] = cum
    cum_t[...] = pad[...].T[:heads]
    pad[:, :heads] = deltas
    dt_t[...] = pad[...].T[:heads]

    @pl.when(me == 0)
    def _():
        xh[...] = jnp.zeros_like(xh)
        bh[...] = jnp.zeros_like(bh)

    @pl.when(me > 0)
    def _():
        for copy in halo_copies():
            copy.wait_recv()

    bs[0:8] = bh[...].astype(F32)[HALO - 8 :]
    bs[8:] = bc_ref[...].astype(F32)
    for g in range(groups):
        span = slice(g * 2 * state, (g + 1) * 2 * state)
        total = cbc_ref[0, g : g + 1, :] * bs[base : base + tokens, span]
        for k in range(1, taps):
            total = total + cbc_ref[k, g : g + 1, :] * bs[base + k : base + k + tokens, span]
        act = silu(total)
        b_part = act[:, :state].astype(BF16)
        c_part = act[:, state:].astype(BF16)
        c_act[g] = c_part
        b_t[g] = b_part.astype(F32).T.astype(BF16)
        product = lax.dot_general(
            c_part, b_part, (((1,), (1,)), ((), ())), preferred_element_type=F32
        )
        inter[g] = jnp.where(causal, product, 0.0)

    head_of_lane = lax.broadcasted_iota(jnp.int32, (tokens, wide), 1) // head_dim

    def spread(columns):
        result = jnp.broadcast_to(columns[:, per_chunk - 1 :], (tokens, wide))
        for h in range(per_chunk - 2, -1, -1):
            result = jnp.where(head_of_lane == h, columns[:, h : h + 1], result)
        return result

    def make_state(k, carry):
        g = k // group_chunks
        cols = pl.ds(pl.multiple_of(k * wide, wide), wide)
        xs[0:8] = xh[:, cols].astype(F32)[HALO - 8 :]
        xs[8:] = x_ref[:, cols].astype(F32)
        weights = cx_ref[:, cols]
        total = weights[0:1] * xs[base : base + tokens]
        for i in range(1, taps):
            total = total + weights[i : i + 1] * xs[base + i : base + i + tokens]
        act = silu(total).astype(BF16)
        xact[k] = act
        ec[k] = jnp.exp(spread(col_cum[k]))
        scaled = (spread(col_tail[k]) * act.astype(F32)).astype(BF16)
        made = jnp.dot(b_t[g], scaled, preferred_element_type=F32)
        own[k] = made

        @pl.when((me == 0) & (me < n - 1))
        def _():
            sendb[k] = made.astype(BF16)
            state_copy(k).start()

        return carry

    lax.fori_loop(0, chunks, make_state, 0)

    def group_step(g, carry):
        def chunk_step(j, squares):
            k = g * group_chunks + j
            cols = pl.ds(pl.multiple_of(k * wide, wide), wide)

            @pl.when(me > 0)
            def _():
                state_copy(k).wait_recv()

            @pl.when((me > 0) & (me < n - 1))
            def _():
                decay = ec[k, tokens - 1 : tokens, :]
                sendb[k] = (decay * recvb[k].astype(F32) + own[k]).astype(BF16)
                state_copy(k).start()

            act = xact[k]
            columns = col_cum[k]
            parts = []
            skips = jnp.zeros((1, wide), F32)
            for h in range(per_chunk):
                at = k * per_chunk + h
                gap = jnp.minimum(columns[:, h : h + 1] - cum_t[pl.ds(at, 1), :], 0.0)
                weight = (jnp.exp(gap) * dt_t[pl.ds(at, 1), :] * inter[g]).astype(BF16)
                parts.append(
                    jnp.dot(
                        weight, act[:, h * head_dim : (h + 1) * head_dim],
                        preferred_element_type=F32,
                    )
                )
                skips = jnp.where(head_of_lane[0:1] == h, ds_ref[at], skips)
            gated[k] = jnp.concatenate(parts, axis=1) + skips * act.astype(F32)

            @pl.when(me > 0)
            def _():
                gated[k] += ec[k] * jnp.dot(c_act[g], recvb[k], preferred_element_type=F32)

            done = gated[k] * silu(z_ref[:, cols].astype(F32))
            gated[k] = done
            return squares + jnp.sum(done * done, axis=1, keepdims=True)

        squares = lax.fori_loop(0, group_chunks, chunk_step, jnp.zeros((tokens, 1), F32))
        scale = lax.rsqrt(squares * (groups / width) + EPS)

        def finish(j, carry):
            k = g * group_chunks + j
            cols = pl.ds(pl.multiple_of(k * wide, wide), wide)
            o_ref[:, cols] = (gated[k] * scale * gain_ref[:, cols]).astype(BF16)
            return carry

        return lax.fori_loop(0, group_chunks, finish, carry)

    lax.fori_loop(0, groups, group_step, 0)

    @pl.when(me < n - 1)
    def _():
        for copy in halo_copies():
            copy.wait_send()

        def drain(k, carry):
            state_copy(k).wait_send()
            return carry

        lax.fori_loop(0, chunks, drain, 0)


def shards(x_in, bc_in, z_in, dt_raw, conv_x, conv_bc, a_log, d_skip, norm_gain):
    tokens, width = x_in.shape
    assert tokens == BLOCK
    groups = bc_in.shape[1]
    heads = dt_raw.shape[1]
    state = bc_in.shape[2] // 2
    head_dim = width // heads
    per_chunk = min(HEADS_PER_CHUNK, heads // groups)
    wide = per_chunk * head_dim
    chunks = width // wide
    n = lax.axis_size("seq")
    vmem = pl.BlockSpec(memory_space=pltpu.VMEM)
    smem = pl.BlockSpec(memory_space=pltpu.SMEM)
    V = pltpu.VMEM
    dma = pltpu.SemaphoreType.DMA
    return pl.pallas_call(
        functools.partial(kernel, n, groups, heads),
        out_shape=jax.ShapeDtypeStruct((tokens, width), BF16),
        in_specs=[vmem] * 7 + [smem, vmem],
        out_specs=vmem,
        scratch_shapes=[
            V((HALO, width), BF16),
            V((HALO, groups * 2 * state), BF16),
            V((chunks, state, wide), BF16),
            V((chunks, state, wide), BF16),
            V((chunks, state, wide), F32),
            V((chunks, tokens, wide), F32),
            V((chunks, tokens, wide), F32),
            V((tokens + 8, wide), F32),
            V((tokens + 8, groups * 2 * state), F32),
            V((chunks, tokens, wide), BF16),
            V((heads, tokens), F32),
            V((heads, tokens), F32),
            V((chunks, tokens, per_chunk), F32),
            V((chunks, tokens, per_chunk), F32),
            V((tokens, 128), F32),
            V((groups, tokens, tokens), F32),
            V((groups, tokens, state), BF16),
            V((groups, state, tokens), BF16),
            dma((2,)),
            dma((2,)),
            dma((chunks,)),
            dma((chunks,)),
        ],
        compiler_params=pltpu.CompilerParams(
            collective_id=0, has_side_effects=True, vmem_limit_bytes=40 * 1024 * 1024
        ),
    )(
        x_in, bc_in.reshape(tokens, groups * 2 * state), z_in, dt_raw, conv_x, conv_bc,
        a_log.reshape(1, heads), d_skip, norm_gain.reshape(1, width),
    )


def solution(mesh):
    return jax.shard_map(
        shards,
        mesh=mesh,
        in_specs=(
            P(("groups", "seq"), "head"),
            P(("groups", "seq"), "head", None),
            P(("groups", "seq"), "head"),
            P(("groups", "seq"), "head"),
            P(None, "head"),
            P(None, "head", None),
            P("head"),
            P("head"),
            P("head"),
        ),
        out_specs=P(("groups", "seq"), "head"),
        check_vma=False,
    )
```

time: 106 us -> 29.7 us (0.28)
  the two profiles are of different devices: /device:TPU:0 before, /device:TPU:24 now
where the time goes in v1:
time: 29.7 us; the launch traced here: 29.4 us
  Pallas kernels  24.1 us (81%)
  local copies, waits for them, and re-layouts  5.27 us (18%)
    pallas_call x1, Pallas kernels, shards(): pl.pallas_call(functools.partial(kernel, n, groups, heads), out_shape=jax...  24.1 us
    unnamed x17, local copies, waits for them, and re-layouts  5.27 us

profile of v1, /device:TPU:24, one launch (start us, length us, event | category | flops | bytes accessed | tf_op | source)
XLA Modules:
  0.0 29.4 jit_solution(145582457644951937)
XLA Ops:
  0.0 0.8 %copy.10.dt_ref = f32[128,32]{1,0:T(8,128)S(1)} copy(f32[128,32]{0,1:T(8,128)} %param.12) | data formatting | bytes 32768 | tf_op args[3]
  0.8 0.0 copy-start.2
  0.8 0.0 copy-start.3
  0.8 0.0 copy-start.4
  0.8 0.9 %copy.11 = bf16[16,8,2,256]{3,1,2,0:T(8,128)(2,1)S(1)} copy(bf16[16,8,2,256]{3,2,1,0:T(2,128)(2,1)} %bitcast.7) | data formatting | bytes 262144
  1.8 0.0 copy-start.5
  1.8 0.0 copy-start.6
  1.8 0.0 copy-done.2
  1.8 0.0 copy-done.3
  1.8 0.0 copy-done.4
  1.8 0.6 %copy-done.5 = f32[32]{0:T(128)S(1)} copy-done((f32[32]{0:T(128)S(1)}, f32[32]{0:T(128)}, u32[]{:S(2)}) %copy-start.5) | copy-done | bytes 152
  2.4 0.0 copy-done.6
  2.5 0.0 copy-start
  2.5 1.0 %copy-done = bf16[128,2048]{1,0:T(8,128)(2,1)S(1)} copy-done((bf16[128,2048]{1,0:T(8,128)(2,1)S(1)}, bf16[128,2048]{1,0:T(8,128)(2,1)}, u32[]{:S(2)}) %copy-start) | copy-done | bytes 524312
  3.5 0.0 copy-start.1
  3.5 1.0 %copy-done.1 = bf16[128,2048]{1,0:T(8,128)(2,1)S(1)} copy-done((bf16[128,2048]{1,0:T(8,128)(2,1)S(1)}, bf16[128,2048]{1,0:T(8,128)(2,1)}, u32[]{:S(2)}) %copy-start.1) | copy-done | bytes 524312
  4.5 24.1 %shard_map.91 = bf16[128,2048]{1,0:T(8,128)(2,1)S(1)} custom-call(bf16[128,2048]{1,0:T(8,128)(2,1)S(1)} %copy-done, bf16[128,512]{1,0:T(8,128)(2,1)S(1)} %bitcast.4, bf16[128,2048]{1,0:T(8,128)(2,1)S(1)} %copy-done.1, f32[128,32]{1,0:T(8,128)S(1)} %copy.10.dt_ref, f32[4,2048]{1,0:T(4,128)S(1)} %copy-done.2, f32[4,2,256]{2,1,0:T(2,128)S(1)} %copy-done.3, ...), custom_call_target="tpu_custom_call" | custom-call | tf_op jit(solution)/shard_map/pallas_call | solution.py:228
  28.7 0.8 %copy.13 = bf16[128,2048]{1,0:T(8,128)(2,1)} copy(bf16[128,2048]{1,0:T(8,128)(2,1)S(1)} %shard_map.91) | data formatting | bytes 1048576
Async XLA Ops:
  0.8 1.0 %copy-start.2 = (f32[4,2048]{1,0:T(4,128)S(1)}, f32[4,2048]{1,0:T(4,128)}, u32[]{:S(2)}) copy-start(f32[4,2048]{1,0:T(4,128)} %cx_ref.1) | copy-start | bytes 98308
  0.8 1.0 %copy-start.3 = (f32[4,2,256]{2,1,0:T(2,128)S(1)}, f32[4,2,256]{2,1,0:T(2,128)}, u32[]{:S(2)}) copy-start(f32[4,2,256]{2,1,0:T(2,128)} %cbc_ref.1) | copy-start | bytes 24580
  0.8 1.0 %copy-start.4 = (f32[2048]{0:T(1024)S(1)}, f32[2048]{0:T(1024)}, u32[]{:S(2)}) copy-start(f32[2048]{0:T(1024)} %param.17) | copy-start | bytes 24580
  1.8 0.7 %copy-start.5 = (f32[32]{0:T(128)S(1)}, f32[32]{0:T(128)}, u32[]{:S(2)}) copy-start(f32[32]{0:T(128)} %param.15) | copy-start | bytes 388
  1.8 0.7 %copy-start.6 = (f32[32]{0:T(128)S(1)}, f32[32]{0:T(128)}, u32[]{:S(2)}) copy-start(f32[32]{0:T(128)} %ds_ref.1) | copy-start | bytes 388
  2.5 1.0 %copy-start = (bf16[128,2048]{1,0:T(8,128)(2,1)S(1)}, bf16[128,2048]{1,0:T(8,128)(2,1)}, u32[]{:S(2)}) copy-start(bf16[128,2048]{1,0:T(8,128)(2,1)} %x_ref.1) | copy-start | bytes 1572868
  3.5 1.0 %copy-start.1 = (bf16[128,2048]{1,0:T(8,128)(2,1)S(1)}, bf16[128,2048]{1,0:T(8,128)(2,1)}, u32[]{:S(2)}) copy-start(bf16[128,2048]{1,0:T(8,128)(2,1)} %z_ref.1) | copy-start | bytes 1572868

commit v2 on v1

--- a/solution.py
+++ b/solution.py
@@ -10,6 +10,7 @@
 BLOCK = 128
 EPS = 1e-05
 HALO = 16
+LIMIT = 66400000
 HEADS_PER_CHUNK = 4
 F32 = jnp.float32
 BF16 = jnp.bfloat16
@@ -22,17 +23,17 @@
 
 
 def kernel(
-    n, groups, heads, x_ref, bc_ref, z_ref, dt_ref, cx_ref, cbc_ref, al_ref, ds_ref, gain_ref,
-    o_ref, xh, bh, sendb, recvb, own, gated, ec, xs, bs, xact, cum_t, dt_t, col_cum, col_tail,
-    pad, inter, c_act, b_t, h_send, h_recv, s_send, s_recv,
+    n, groups, heads, x_hbm, bc_hbm, z_hbm, dt_hbm, cx_hbm, cbc_hbm, al_hbm, ds_hbm, gain_hbm,
+    o_ref, x_ref, bc_ref, z_ref, dt_ref, cx_ref, cbc_ref, al_ref, ds_ref, gain_ref, xh, bh, sendb, recvb, own, gated, ec, xs, bs, xact, cum_t, dt_t, col_cum, col_tail,
+    pad, square, inter, c_act, b_t, h_send, h_recv, s_send, s_recv, x_sem, z_sem, p_sem,
 ):
-    tokens, width = x_ref.shape
+    tokens, width = x_hbm.shape
     head_dim = width // heads
     per_chunk = xact.shape[2] // head_dim
     wide = xact.shape[2]
     chunks = width // wide
     group_chunks = chunks // groups
-    state = bc_ref.shape[1] // groups // 2
+    state = bc_hbm.shape[1] // groups // 2
     taps = cx_ref.shape[0]
     base = 8 - (taps - 1)
     me = lax.axis_index("seq")
@@ -44,7 +45,7 @@
                 src_ref=src.at[rows], dst_ref=dst, send_sem=h_send.at[i], recv_sem=h_recv.at[i],
                 device_id={"seq": me + 1}, device_id_type=MESH,
             )
-            for i, (src, dst) in enumerate(((bc_ref, bh), (x_ref, xh)))
+            for i, (src, dst) in enumerate(((bc_hbm, bh), (x_hbm, xh)))
         ]
 
     def state_copy(k):
@@ -53,11 +54,40 @@
             recv_sem=s_recv.at[k], device_id={"seq": me + 1}, device_id_type=MESH,
         )
 
+    def columns_of(k):
+        return pl.ds(pl.multiple_of(k * wide, wide), wide)
+
+    def x_copy(k):
+        return pltpu.make_async_copy(x_hbm.at[:, columns_of(k)], x_ref.at[k], x_sem.at[k])
+
+    def z_copy(k):
+        return pltpu.make_async_copy(z_hbm.at[:, columns_of(k)], z_ref.at[k], z_sem.at[k])
+
+    pairs = (
+        (dt_hbm, dt_ref), (al_hbm, al_ref), (cbc_hbm, cbc_ref), (cx_hbm, cx_ref),
+        (ds_hbm, ds_ref), (gain_hbm, gain_ref), (bc_hbm, bc_ref),
+    )
+    small = [pltpu.make_async_copy(a, b, p_sem.at[i]) for i, (a, b) in enumerate(pairs)]
+
     barrier = pltpu.get_barrier_semaphore()
 
     @pl.when(me > 0)
     def _():
         pl.semaphore_signal(barrier, inc=1, device_id={"seq": me - 1}, device_id_type=MESH)
+
+    for copy in small:
+        copy.start()
+
+    def fetch_x(k, carry):
+        x_copy(k).start()
+        return carry
+
+    def fetch_z(k, carry):
+        z_copy(k).start()
+        return carry
+
+    lax.fori_loop(0, chunks, fetch_x, 0)
+    lax.fori_loop(0, chunks, fetch_z, 0)
 
     @pl.when(me < n - 1)
     def _():
@@ -68,8 +98,14 @@
     row = lax.broadcasted_iota(jnp.int32, (tokens, tokens), 0)
     col = lax.broadcasted_iota(jnp.int32, (tokens, tokens), 1)
     causal = row >= col
+    small[0].wait()
+    small[1].wait()
     raw = dt_ref[...]
-    deltas = jnp.maximum(raw, 0.0) + jnp.log1p(jnp.exp(-jnp.abs(raw)))
+    softplus = jnp.maximum(raw, 0.0) + jnp.log1p(jnp.exp(-jnp.abs(raw)))
+    dt_t[...] = softplus
+    pad[...] = jnp.zeros_like(pad)
+    pad[:heads] = softplus
+    deltas = pad[...].T[:, :heads]
     rates = -jnp.exp(al_ref[...]) * deltas
     cum = jnp.dot(
         causal.astype(F32), rates, precision=lax.Precision.HIGHEST, preferred_element_type=F32
@@ -79,11 +115,9 @@
         part = slice(k * per_chunk, (k + 1) * per_chunk)
         col_cum[k] = cum[:, part]
         col_tail[k] = tail[:, part]
-    pad[...] = jnp.zeros_like(pad)
-    pad[:, :heads] = cum
-    cum_t[...] = pad[...].T[:heads]
-    pad[:, :heads] = deltas
-    dt_t[...] = pad[...].T[:heads]
+    square[...] = jnp.zeros_like(square)
+    square[:, :heads] = cum
+    cum_t[...] = square[...].T[:heads]
 
     @pl.when(me == 0)
     def _():
@@ -95,6 +129,8 @@
         for copy in halo_copies():
             copy.wait_recv()
 
+    small[2].wait()
+    small[6].wait()
     bs[0:8] = bh[...].astype(F32)[HALO - 8 :]
     bs[8:] = bc_ref[...].astype(F32)
     for g in range(groups):
@@ -120,11 +156,15 @@
             result = jnp.where(head_of_lane == h, columns[:, h : h + 1], result)
         return result
 
+    for copy in small[3:6]:
+        copy.wait()
+
     def make_state(k, carry):
         g = k // group_chunks
-        cols = pl.ds(pl.multiple_of(k * wide, wide), wide)
+        cols = columns_of(k)
+        x_copy(k).wait()
         xs[0:8] = xh[:, cols].astype(F32)[HALO - 8 :]
-        xs[8:] = x_ref[:, cols].astype(F32)
+        xs[8:] = x_ref[k].astype(F32)
         weights = cx_ref[:, cols]
         total = weights[0:1] * xs[base : base + tokens]
         for i in range(1, taps):
@@ -148,18 +188,6 @@
     def group_step(g, carry):
         def chunk_step(j, squares):
             k = g * group_chunks + j
-            cols = pl.ds(pl.multiple_of(k * wide, wide), wide)
-
-            @pl.when(me > 0)
-            def _():
-                state_copy(k).wait_recv()
-
-            @pl.when((me > 0) & (me < n - 1))
-            def _():
-                decay = ec[k, tokens - 1 : tokens, :]
-                sendb[k] = (decay * recvb[k].astype(F32) + own[k]).astype(BF16)
-                state_copy(k).start()
-
             act = xact[k]
             columns = col_cum[k]
             parts = []
@@ -177,11 +205,24 @@
                 skips = jnp.where(head_of_lane[0:1] == h, ds_ref[at], skips)
             gated[k] = jnp.concatenate(parts, axis=1) + skips * act.astype(F32)
 
+            z_copy(k).wait()
+            gate = silu(z_ref[k].astype(F32))
+
+            @pl.when(me > 0)
+            def _():
+                state_copy(k).wait_recv()
+
+            @pl.when((me > 0) & (me < n - 1))
+            def _():
+                decay = ec[k, tokens - 1 : tokens, :]
+                sendb[k] = (decay * recvb[k].astype(F32) + own[k]).astype(BF16)
+                state_copy(k).start()
+
             @pl.when(me > 0)
             def _():
                 gated[k] += ec[k] * jnp.dot(c_act[g], recvb[k], preferred_element_type=F32)
 
-            done = gated[k] * silu(z_ref[:, cols].astype(F32))
+            done = gated[k] * gate
             gated[k] = done
             return squares + jnp.sum(done * done, axis=1, keepdims=True)
 
@@ -190,7 +231,7 @@
 
         def finish(j, carry):
             k = g * group_chunks + j
-            cols = pl.ds(pl.multiple_of(k * wide, wide), wide)
+            cols = columns_of(k)
             o_ref[:, cols] = (gated[k] * scale * gain_ref[:, cols]).astype(BF16)
             return carry
 
@@ -222,15 +263,24 @@
     chunks = width // wide
     n = lax.axis_size("seq")
     vmem = pl.BlockSpec(memory_space=pltpu.VMEM)
-    smem = pl.BlockSpec(memory_space=pltpu.SMEM)
+    hbm = pl.BlockSpec(memory_space=pltpu.HBM)
     V = pltpu.VMEM
     dma = pltpu.SemaphoreType.DMA
     return pl.pallas_call(
         functools.partial(kernel, n, groups, heads),
         out_shape=jax.ShapeDtypeStruct((tokens, width), BF16),
-        in_specs=[vmem] * 7 + [smem, vmem],
+        in_specs=[hbm] * 9,
         out_specs=vmem,
         scratch_shapes=[
+            V((chunks, tokens, wide), BF16),
+            V((tokens, groups * 2 * state), BF16),
+            V((chunks, tokens, wide), BF16),
+            V((heads, tokens), F32),
+            V(conv_x.shape, F32),
+            V(conv_bc.shape, F32),
+            V((1, heads), F32),
+            pltpu.SMEM((heads,), F32),
+            V((1, width), F32),
             V((HALO, width), BF16),
             V((HALO, groups * 2 * state), BF16),
             V((chunks, state, wide), BF16),
@@ -245,6 +295,7 @@
             V((heads, tokens), F32),
             V((chunks, tokens, per_chunk), F32),
             V((chunks, tokens, per_chunk), F32),
+            V((128, tokens), F32),
             V((tokens, 128), F32),
             V((groups, tokens, tokens), F32),
             V((groups, tokens, state), BF16),
@@ -253,12 +304,15 @@
             dma((2,)),
             dma((chunks,)),
             dma((chunks,)),
+            dma((chunks,)),
+            dma((chunks,)),
+            dma((7,)),
         ],
         compiler_params=pltpu.CompilerParams(
-            collective_id=0, has_side_effects=True, vmem_limit_bytes=40 * 1024 * 1024
+            collective_id=0, has_side_effects=True, vmem_limit_bytes=LIMIT
         ),
     )(
-        x_in, bc_in.reshape(tokens, groups * 2 * state), z_in, dt_raw, conv_x, conv_bc,
+        x_in, bc_in.reshape(tokens, groups * 2 * state), z_in, dt_raw.T, conv_x, conv_bc,
         a_log.reshape(1, heads), d_skip, norm_gain.reshape(1, width),
     )
 

time: 29.7 us -> 28 us (0.943)
  local copies, waits for them, and re-layouts: 5.27 us -> 3.45 us
  Pallas kernels: 24.1 us -> 24.4 us
    unnamed x17 -> x2, local copies, waits for them, and re-layouts: 5.27 us -> 3.45 us
where the time goes in v2:
time: 28 us; the launch traced here: 27.8 us
  Pallas kernels  24.4 us (87%)
  local copies, waits for them, and re-layouts  3.45 us (12%)
    pallas_call x1, Pallas kernels, shards(): pl.pallas_call(functools.partial(kernel, n, groups, heads), out_shape=jax...  24.4 us
    unnamed x2, local copies, waits for them, and re-layouts  3.45 us

profile of v2, /device:TPU:24, one launch (start us, length us, event | category | flops | bytes accessed | tf_op | source)
XLA Modules:
  0.0 27.8 jit_solution(8765730563217364734)
XLA Ops:
  0.0 1.6 %copy.10 = bf16[16,8,2,256]{3,1,2,0:T(8,128)(2,1)} copy(bf16[16,8,2,256]{3,2,1,0:T(2,128)(2,1)} %bitcast.6) | data formatting | bytes 262144
  1.6 24.4 %shard_map.91 = bf16[128,2048]{1,0:T(8,128)(2,1)} custom-call(bf16[128,2048]{1,0:T(8,128)(2,1)} %x_hbm.1, bf16[128,512]{1,0:T(8,128)(2,1)} %bitcast.5, bf16[128,2048]{1,0:T(8,128)(2,1)} %z_hbm.1, f32[32,128]{1,0:T(8,128)} %bitcast.7, f32[4,2048]{1,0:T(4,128)} %cx_hbm.1, f32[4,2,256]{2,1,0:T(2,128)} %cbc_hbm.1, f32[1,32]{1,0:T(1,128)} %bitcast.9, f32[32]{0:T(128)} %ds_hbm.1, ...), custom_call_target="tpu_custom_call" | custom-call | tf_op jit(solution)/shard_map/pallas_call | solution.py:269
  26.0 1.9 %copy.12 = bf16[128,2048]{1,0:T(8,128)(2,1)} copy(bf16[128,2048]{1,0:T(8,128)(2,1)} %shard_map.91) | data formatting | bytes 1048576

commit v3 on v2

--- a/solution.py
+++ b/solution.py
@@ -10,7 +10,7 @@
 BLOCK = 128
 EPS = 1e-05
 HALO = 16
-LIMIT = 66400000
+LIMIT = 55000000
 HEADS_PER_CHUNK = 4
 F32 = jnp.float32
 BF16 = jnp.bfloat16
@@ -87,7 +87,6 @@
         return carry
 
     lax.fori_loop(0, chunks, fetch_x, 0)
-    lax.fori_loop(0, chunks, fetch_z, 0)
 
     @pl.when(me < n - 1)
     def _():
@@ -119,6 +118,8 @@
     square[:, :heads] = cum
     cum_t[...] = square[...].T[:heads]
 
+    lax.fori_loop(0, chunks, fetch_z, 0)
+
     @pl.when(me == 0)
     def _():
         xh[...] = jnp.zeros_like(xh)
@@ -159,8 +160,7 @@
     for copy in small[3:6]:
         copy.wait()
 
-    def make_state(k, carry):
-        g = k // group_chunks
+    def make_state(g, k):
         cols = columns_of(k)
         x_copy(k).wait()
         xs[0:8] = xh[:, cols].astype(F32)[HALO - 8 :]
@@ -181,13 +181,11 @@
             sendb[k] = made.astype(BF16)
             state_copy(k).start()
 
-        return carry
-
-    lax.fori_loop(0, chunks, make_state, 0)
 
     def group_step(g, carry):
         def chunk_step(j, squares):
             k = g * group_chunks + j
+            make_state(g, k)
             act = xact[k]
             columns = col_cum[k]
             parts = []

time: 28 us -> 26 us (0.929)
  Pallas kernels: 24.4 us -> 22.3 us
    pallas_call x1, Pallas kernels: 24.4 us -> 22.3 us  [shards(): pl.pallas_call(functools.partial(kernel, n, groups, heads), out_shape=jax...]
    unnamed x2 -> x16, local copies, waits for them, and re-layouts: 3.45 us -> 3.43 us
where the time goes in v3:
time: 26 us; the launch traced here: 25.8 us
  Pallas kernels  22.3 us (86%)
  local copies, waits for them, and re-layouts  3.43 us (13%)
    pallas_call x1, Pallas kernels, shards(): pl.pallas_call(functools.partial(kernel, n, groups, heads), out_shape=jax...  22.3 us
    unnamed x16, local copies, waits for them, and re-layouts  3.43 us

profile of v3, /device:TPU:24, one launch (start us, length us, event | category | flops | bytes accessed | tf_op | source)
XLA Modules:
  0.0 25.8 jit_solution(1850562770080535819)
XLA Ops:
  0.0 0.0 copy-start.1
  0.0 0.0 copy-start.2
  0.0 0.0 copy-start.3
  0.0 0.0 copy-start.4
  0.0 1.0 %copy.10 = bf16[16,8,2,256]{3,1,2,0:T(8,128)(2,1)S(1)} copy(bf16[16,8,2,256]{3,2,1,0:T(2,128)(2,1)} %bitcast.9) | data formatting | bytes 262144
  1.0 0.0 copy-start.5
  1.0 0.0 copy-start.6
  1.0 0.0 copy-done.1
  1.0 0.0 copy-done.2
  1.0 0.0 copy-done.3
  1.0 0.0 copy-done.4
  1.1 0.6 %copy-done.5 = f32[32]{0:T(128)S(1)} copy-done((f32[32]{0:T(128)S(1)}, f32[32]{0:T(128)}, u32[]{:S(2)}) %copy-start.5) | copy-done | bytes 152
  1.6 0.0 copy-done.6
  1.7 0.0 copy-start
  1.7 1.0 %copy-done = bf16[128,2048]{1,0:T(8,128)(2,1)S(1)} copy-done((bf16[128,2048]{1,0:T(8,128)(2,1)S(1)}, bf16[128,2048]{1,0:T(8,128)(2,1)}, u32[]{:S(2)}) %copy-start) | copy-done | bytes 524312
  2.7 22.3 %shard_map.91 = bf16[128,2048]{1,0:T(8,128)(2,1)S(1)} custom-call(bf16[128,2048]{1,0:T(8,128)(2,1)S(1)} %copy-done, bf16[128,512]{1,0:T(8,128)(2,1)S(1)} %bitcast.5, bf16[128,2048]{1,0:T(8,128)(2,1)} %z_hbm.1, f32[32,128]{1,0:T(8,128)S(1)} %bitcast.6, f32[4,2048]{1,0:T(4,128)S(1)} %copy-done.1, f32[4,2,256]{2,1,0:T(2,128)S(1)} %copy-done.3, ...), custom_call_target="tpu_custom_call" | custom-call | tf_op jit(solution)/shard_map/pallas_call | solution.py:267
  25.0 0.8 %copy.12 = bf16[128,2048]{1,0:T(8,128)(2,1)} copy(bf16[128,2048]{1,0:T(8,128)(2,1)S(1)} %shard_map.91) | data formatting | bytes 1048576
Async XLA Ops:
  0.0 1.0 %copy-start.1 = (f32[4,2048]{1,0:T(4,128)S(1)}, f32[4,2048]{1,0:T(4,128)}, u32[]{:S(2)}) copy-start(f32[4,2048]{1,0:T(4,128)} %cx_hbm.1) | copy-start | bytes 98308
  0.0 1.0 %copy-start.2 = (f32[128,32]{0,1:T(8,128)S(1)}, f32[128,32]{0,1:T(8,128)}, u32[]{:S(2)}) copy-start(f32[128,32]{0,1:T(8,128)} %param.12) | copy-start | bytes 49156
  0.0 1.0 %copy-start.3 = (f32[4,2,256]{2,1,0:T(2,128)S(1)}, f32[4,2,256]{2,1,0:T(2,128)}, u32[]{:S(2)}) copy-start(f32[4,2,256]{2,1,0:T(2,128)} %cbc_hbm.1) | copy-start | bytes 24580
  0.0 1.0 %copy-start.4 = (f32[2048]{0:T(1024)S(1)}, f32[2048]{0:T(1024)}, u32[]{:S(2)}) copy-start(f32[2048]{0:T(1024)} %param.17) | copy-start | bytes 24580
  1.0 0.7 %copy-start.5 = (f32[32]{0:T(128)S(1)}, f32[32]{0:T(128)}, u32[]{:S(2)}) copy-start(f32[32]{0:T(128)} %param.15) | copy-start | bytes 388
  1.0 0.7 %copy-start.6 = (f32[32]{0:T(128)S(1)}, f32[32]{0:T(128)}, u32[]{:S(2)}) copy-start(f32[32]{0:T(128)} %ds_hbm.1) | copy-start | bytes 388
  1.7 1.0 %copy-start = (bf16[128,2048]{1,0:T(8,128)(2,1)S(1)}, bf16[128,2048]{1,0:T(8,128)(2,1)}, u32[]{:S(2)}) copy-start(bf16[128,2048]{1,0:T(8,128)(2,1)} %x_hbm.1) | copy-start | bytes 1572868

commit v4 on v3

--- a/solution.py
+++ b/solution.py
@@ -186,6 +186,17 @@
         def chunk_step(j, squares):
             k = g * group_chunks + j
             make_state(g, k)
+
+            @pl.when(me > 0)
+            def _():
+                state_copy(k).wait_recv()
+
+            @pl.when((me > 0) & (me < n - 1))
+            def _():
+                decay = ec[k, tokens - 1 : tokens, :]
+                sendb[k] = (decay * recvb[k].astype(F32) + own[k]).astype(BF16)
+                state_copy(k).start()
+
             act = xact[k]
             columns = col_cum[k]
             parts = []
@@ -205,16 +216,6 @@
 
             z_copy(k).wait()
             gate = silu(z_ref[k].astype(F32))
-
-            @pl.when(me > 0)
-            def _():
-                state_copy(k).wait_recv()
-
-            @pl.when((me > 0) & (me < n - 1))
-            def _():
-                decay = ec[k, tokens - 1 : tokens, :]
-                sendb[k] = (decay * recvb[k].astype(F32) + own[k]).astype(BF16)
-                state_copy(k).start()
 
             @pl.when(me > 0)
             def _():

time: 26 us -> 26.4 us (1.015)
  Pallas kernels: 22.3 us -> 22.7 us
    pallas_call x1, Pallas kernels: 22.3 us -> 22.7 us  [shards(): pl.pallas_call(functools.partial(kernel, n, groups, heads), out_shape=jax...]
where the time goes in v4:
time: 26.4 us; the launch traced here: 26.2 us
  Pallas kernels  22.7 us (86%)
  local copies, waits for them, and re-layouts  3.43 us (13%)
    pallas_call x1, Pallas kernels, shards(): pl.pallas_call(functools.partial(kernel, n, groups, heads), out_shape=jax...  22.7 us
    unnamed x16, local copies, waits for them, and re-layouts  3.43 us

profile of v4, /device:TPU:24, one launch (start us, length us, event | category | flops | bytes accessed | tf_op | source)
XLA Modules:
  0.0 26.2 jit_solution(4045545069706164426)
XLA Ops:
  0.0 0.0 copy-start.1
  0.0 0.0 copy-start.2
  0.0 0.0 copy-start.3
  0.0 0.0 copy-start.4
  0.0 1.0 %copy.10 = bf16[16,8,2,256]{3,1,2,0:T(8,128)(2,1)S(1)} copy(bf16[16,8,2,256]{3,2,1,0:T(2,128)(2,1)} %bitcast.9) | data formatting | bytes 262144
  1.0 0.0 copy-start.5
  1.0 0.0 copy-start.6
  1.0 0.0 copy-done.1
  1.0 0.0 copy-done.2
  1.0 0.0 copy-done.3
  1.0 0.0 copy-done.4
  1.1 0.6 %copy-done.5 = f32[32]{0:T(128)S(1)} copy-done((f32[32]{0:T(128)S(1)}, f32[32]{0:T(128)}, u32[]{:S(2)}) %copy-start.5) | copy-done | bytes 152
  1.6 0.0 copy-done.6
  1.7 0.0 copy-start
  1.7 1.0 %copy-done = bf16[128,2048]{1,0:T(8,128)(2,1)S(1)} copy-done((bf16[128,2048]{1,0:T(8,128)(2,1)S(1)}, bf16[128,2048]{1,0:T(8,128)(2,1)}, u32[]{:S(2)}) %copy-start) | copy-done | bytes 524312
  2.7 22.7 %shard_map.91 = bf16[128,2048]{1,0:T(8,128)(2,1)S(1)} custom-call(bf16[128,2048]{1,0:T(8,128)(2,1)S(1)} %copy-done, bf16[128,512]{1,0:T(8,128)(2,1)S(1)} %bitcast.5, bf16[128,2048]{1,0:T(8,128)(2,1)} %z_hbm.1, f32[32,128]{1,0:T(8,128)S(1)} %bitcast.6, f32[4,2048]{1,0:T(4,128)S(1)} %copy-done.1, f32[4,2,256]{2,1,0:T(2,128)S(1)} %copy-done.3, ...), custom_call_target="tpu_custom_call" | custom-call | tf_op jit(solution)/shard_map/pallas_call | solution.py:268
  25.4 0.8 %copy.12 = bf16[128,2048]{1,0:T(8,128)(2,1)} copy(bf16[128,2048]{1,0:T(8,128)(2,1)S(1)} %shard_map.91) | data formatting | bytes 1048576
Async XLA Ops:
  0.0 1.0 %copy-start.1 = (f32[4,2048]{1,0:T(4,128)S(1)}, f32[4,2048]{1,0:T(4,128)}, u32[]{:S(2)}) copy-start(f32[4,2048]{1,0:T(4,128)} %cx_hbm.1) | copy-start | bytes 98308
  0.0 1.0 %copy-start.2 = (f32[128,32]{0,1:T(8,128)S(1)}, f32[128,32]{0,1:T(8,128)}, u32[]{:S(2)}) copy-start(f32[128,32]{0,1:T(8,128)} %param.12) | copy-start | bytes 49156
  0.0 1.0 %copy-start.3 = (f32[4,2,256]{2,1,0:T(2,128)S(1)}, f32[4,2,256]{2,1,0:T(2,128)}, u32[]{:S(2)}) copy-start(f32[4,2,256]{2,1,0:T(2,128)} %cbc_hbm.1) | copy-start | bytes 24580
  0.0 1.0 %copy-start.4 = (f32[2048]{0:T(1024)S(1)}, f32[2048]{0:T(1024)}, u32[]{:S(2)}) copy-start(f32[2048]{0:T(1024)} %param.17) | copy-start | bytes 24580
  1.0 0.7 %copy-start.5 = (f32[32]{0:T(128)S(1)}, f32[32]{0:T(128)}, u32[]{:S(2)}) copy-start(f32[32]{0:T(128)} %param.15) | copy-start | bytes 388
  1.0 0.7 %copy-start.6 = (f32[32]{0:T(128)S(1)}, f32[32]{0:T(128)}, u32[]{:S(2)}) copy-start(f32[32]{0:T(128)} %ds_hbm.1) | copy-start | bytes 388
  1.7 1.0 %copy-start = (bf16[128,2048]{1,0:T(8,128)(2,1)S(1)}, bf16[128,2048]{1,0:T(8,128)(2,1)}, u32[]{:S(2)}) copy-start(bf16[128,2048]{1,0:T(8,128)(2,1)} %x_hbm.1) | copy-start | bytes 1572868
